TPU v7x, 256 devices: a whole 4x4x8 slice. The times are simulated.
256 devices in a mesh: rep: 8 (over z_lo, x), exp: 32 (over y, z_hi, core).
Axes of the slice: x: 4, y: 4, z: 8 (z_hi: 4, z_lo: 2; z = z_hi * 2 + z_lo), core: 2. Of those that a mesh axis runs over, the one named last changes fastest.
Arguments:
- hidden: bfloat16 [4096, 7168], P(('rep', 'exp')), may hold values from -6 to 6
- expert_ids: int32 [4096, 8], P(('rep', 'exp')), may hold values from 0 to 15, all different within a row; in each aligned block of 16 rows (0 to 15, 16 to 31, ...) at most 10 rows name the same one
- router: bfloat16 [7168, 16], replicated, may hold values from -0.0625 to 0.0625
- gate_up: bfloat16 [32, 512, 2, 7168], P('exp', 'rep'), may hold values from -0.0625 to 0.0625
- down_weight: bfloat16 [32, 512, 7168], P('exp', 'rep'), may hold values from -0.1875 to 0.1875
- query_latent: bfloat16 [4096, 64, 512], P(('rep', 'exp')), may hold values from -110 to 110
- query_rope: bfloat16 [4096, 64, 64], P(('rep', 'exp')), may hold values from -6 to 6
- cache_latent: bfloat16 [4096, 256, 512], P(('rep', 'exp')), may hold values from -8 to 8
- cache_rope: bfloat16 [4096, 64, 256], P(('rep', 'exp')), may hold values from -5 to 5
- lengths: int32 [4096], P(('rep', 'exp')), may hold values from 32 to 256, as said below
Outputs:
- moe_out: bfloat16 [4096, 7168], P(('rep', 'exp'))
- attn_latent: bfloat16 [4096, 64, 512], P(('rep', 'exp'))
Inputs may be any that keep to these rules, and one draw needn't show every extreme that they name: `expert_ids`: in every aligned block of 16 rows no expert is named by more than 10 pairs, a bound that some block reaches. `lengths`: some row has length 256.
All inputs are finite; a program needn't handle non-finite values.
Results may differ from a plain program's by a relative error of at most 0.015.
Values may be sent and summed in bfloat16 or wider, within the bound.
No kernel may reach another device: no remote copies, remote signals or barrier semaphores. Data moves between devices by JAX's collectives and lax.ppermute only.
A program may use at most 128 MiB of HBM per device.

v0:
```python
import math
import jax
import jax.numpy as jnp
from jax import lax
from jax.sharding import PartitionSpec as P

ROPE = 64
NOPE = 128
route_scale = 2.827


def slot_table(expert_ids, experts, capacity):
    flat_ids = expert_ids.reshape(-1)
    onehot = (flat_ids[:, None] == jnp.arange(experts, dtype=jnp.int32)[None, :]).astype(jnp.int32)
    earlier = jnp.cumsum(onehot, axis=0) - onehot
    slot_rank = jnp.sum(earlier * onehot, axis=1)
    return flat_ids * capacity + slot_rank


def bucket_rows(rows_in, flat_slot, experts, capacity):
    row_total = rows_in.shape[0]
    pair_total = flat_slot.shape[0]
    slot_matrix = (
        jnp.arange(experts * capacity, dtype=jnp.int32)[:, None] == flat_slot[None, :]
    ).astype(jnp.float32)
    slot_matrix = jnp.sum(
        slot_matrix.reshape(experts * capacity, row_total, pair_total // row_total), axis=2
    )
    return jnp.dot(
        slot_matrix.astype(jnp.bfloat16), rows_in, preferred_element_type=jnp.float32
    ).astype(jnp.bfloat16)


def partial_output(rows_in, gate_up, down_weight):
    dims = (((1,), (1,)), ((), ()))
    gate_value = lax.dot_general(
        rows_in, gate_up[:, 0, :], dims, preferred_element_type=jnp.float32
    )
    up_value = lax.dot_general(rows_in, gate_up[:, 1, :], dims, preferred_element_type=jnp.float32)
    activated = (jax.nn.silu(gate_value) * up_value).astype(jnp.bfloat16)
    return jnp.dot(activated, down_weight, preferred_element_type=jnp.float32)


def attend(query_latent, query_rope, cache_latent, cache_rope, row_lengths):
    score_scale = 1.0 / math.sqrt(NOPE + ROPE)
    scores = jnp.einsum(
        "rhc,rlc->rhl", query_latent, cache_latent, preferred_element_type=jnp.float32
    )
    scores = scores + jnp.einsum(
        "rhp,rpl->rhl", query_rope, cache_rope, preferred_element_type=jnp.float32
    )
    scores = scores * score_scale
    valid_mask = (
        jnp.arange(cache_latent.shape[1], dtype=jnp.int32)[None, None, :]
        < row_lengths[:, None, None]
    )
    scores = jnp.where(valid_mask, scores, -1e30)
    row_max = jnp.max(scores, axis=2, keepdims=True)
    weights_raw = jnp.where(valid_mask, jnp.exp(scores - row_max), 0.0)
    attn_probs = (weights_raw / jnp.sum(weights_raw, axis=2, keepdims=True)).astype(jnp.bfloat16)
    output = jnp.einsum(
        "rhl,rlc->rhc", attn_probs, cache_latent, preferred_element_type=jnp.float32
    )
    return output.astype(jnp.bfloat16)


def on_device(
    hidden,
    expert_ids,
    router,
    gate_up,
    down_weight,
    query_latent,
    query_rope,
    cache_latent,
    cache_rope,
    lengths,
):
    groups = lax.axis_size("exp")
    experts = groups // 2
    rows_dev = hidden.shape[0]
    top_k = expert_ids.shape[1]
    model_width = hidden.shape[1]
    capacity = min(rows_dev, max(2, rows_dev * top_k * 5 // (4 * experts)))
    full_gate_up, full_down = (
        lax.all_gather(gate_up, "rep", axis=1, tiled=True),
        lax.all_gather(down_weight, "rep", axis=1, tiled=True),
    )
    slice_gate_up = full_gate_up[0]
    slice_down = full_down[0]
    logits = jnp.dot(hidden, router, preferred_element_type=jnp.float32)
    onehot = (expert_ids[:, :, None] == jnp.arange(experts, dtype=jnp.int32)[None, None, :]).astype(
        jnp.float32
    )
    picked = jnp.sum(onehot * logits[:, None, :], axis=2)
    sigmoid_scores = jax.nn.sigmoid(picked)
    mixing = sigmoid_scores / jnp.sum(sigmoid_scores, axis=1, keepdims=True) * route_scale
    flat_slot = slot_table(expert_ids, experts, capacity)
    buckets = bucket_rows(hidden, flat_slot, experts, capacity).reshape(
        experts, capacity, model_width
    )
    outgoing = jnp.broadcast_to(buckets[:, None], (experts, 2, capacity, model_width)).reshape(
        groups, capacity, model_width
    )
    arrived = lax.all_to_all(outgoing, "exp", split_axis=0, concat_axis=0, tiled=True)
    item_total = arrived.shape[1]
    slice_parts = (
        partial_output(arrived.reshape(-1, model_width), slice_gate_up, slice_down)
        .astype(jnp.bfloat16)
        .reshape(groups, item_total, model_width)
    )
    returned = lax.all_to_all(slice_parts, "exp", split_axis=0, concat_axis=0, tiled=True)
    paired = returned.reshape(experts, 2, capacity, model_width).astype(jnp.float32)
    answers = (paired[:, 0] + paired[:, 1]).astype(jnp.bfloat16)
    flat_answers = answers.reshape(experts * capacity, model_width)
    chosen = jnp.take(flat_answers, flat_slot, axis=0).reshape(rows_dev, top_k, model_width)
    moe_out = jnp.sum(chosen.astype(jnp.float32) * mixing[:, :, None], axis=1).astype(jnp.bfloat16)
    attn_latent = attend(query_latent, query_rope, cache_latent, cache_rope, lengths)
    return (moe_out, attn_latent)


def solution(mesh):
    return jax.shard_map(
        on_device,
        mesh=mesh,
        in_specs=(
            P(("rep", "exp"), None),
            P(("rep", "exp"), None),
            P(),
            P("exp", "rep", None, None),
            P("exp", "rep", None),
            P(("rep", "exp"), None, None),
            P(("rep", "exp"), None, None),
            P(("rep", "exp"), None, None),
            P(("rep", "exp"), None, None),
            P(("rep", "exp")),
        ),
        out_specs=(P(("rep", "exp"), None), P(("rep", "exp"), None, None)),
        check_vma=False,
    )
```

profile of v0, /device:TPU:33, one launch (start us, length us, event | category | flops | bytes accessed | tf_op | source)
XLA Modules:
  0.0 641.1 jit_solution(8945141382381900328)
XLA Ops:
  7.2 3.2 copy.25
  10.5 0.7 all-gather.5.cloned.1.call-update
  11.3 0.1 reshape.133
  11.4 0.1 fusion.20
  11.5 0.2 reduce_window_sum.11
  11.6 0.2 select_reduce_fusion.1
  11.9 0.1 convert_reduce_fusion
  12.1 1.7 convolution_convert_fusion.1
  13.8 2.8 broadcast_in_dim.48
  16.5 2.9 broadcast_in_dim.49
  19.5 254.0 %all_to_all.10 = bf16[32,10,7168]{2,1,0:T(8,128)(2,1)} all-to-all(bf16[32,10,7168]{2,1,0:T(8,128)(2,1)S(1)} %bitcast.54), channel_id=1, replica_groups=mesh['rep'=8,'exp'=32] {'exp'}, dimensions={0} | all-to-all | bytes 9175040 | tf_op jit(solution)/shard_map/all_to_all | solution.py:105
  273.5 8.1 %reshape.135 = bf16[320,7168]{1,0:T(8,128)(2,1)} reshape(bf16[32,10,7168]{2,1,0:T(8,128)(2,1)} %all_to_all.10) | data formatting | bytes 9175040 | tf_op jit(solution)/shard_map/reshape | solution.py:108
  281.6 41.4 %all-gather.3.cloned.1.call-done = bf16[1,512,2,7168]{3,1,2,0:T(8,128)(2,1)} async-done(((bf16[1,64,2,7168]{3,1,2,0:T(8,128)(2,1)}), bf16[1,512,2,7168]{3,1,2,0:T(8,128)(2,1)}) %all-gather.3.cloned.1.call-update) | async-done | bytes 14680080 | tf_op jit(solution)/shard_map/all_gather | solution.py:86
  322.9 7.0 %fusion.4 = f32[320,512]{1,0:T(8,128)S(1)} fusion(bf16[320,7168]{1,0:T(8,128)(2,1)} %reshape.135, bf16[512,2,7168]{2,0,1:T(8,128)(2,1)} %bitcast.55), kind=kOutput, calls=%fused_computation.11 | convolution fusion | flops 2348810240 | bytes 12582912 | tf_op jit(solution)/shard_map/dot_general | solution.py:36
  330.0 77.4 %all-gather.5.cloned.1.call-done = bf16[1,512,7168]{2,1,0:T(8,128)(2,1)} async-done(((bf16[1,64,7168]{2,1,0:T(8,128)(2,1)}), bf16[1,512,7168]{2,1,0:T(8,128)(2,1)}) %all-gather.5.cloned.1.call-update) | async-done | bytes 7340048 | tf_op jit(solution)/shard_map/all_gather | solution.py:87
  407.4 13.7 %convolution_convert_fusion = bf16[320,7168]{1,0:T(8,128)(2,1)} fusion(bf16[1,512,7168]{2,1,0:T(8,128)(2,1)} %all-gather.5.cloned.1.call-done, bf16[320,7168]{1,0:T(8,128)(2,1)} %reshape.135, bf16[512,2,7168]{2,0,1:T(8,128)(2,1)} %bitcast.56, f32[320,512]{1,0:T(8,128)S(1)} %fusion.4), kind=kOutput, calls=%fused_computation.2 | convolution fusion | flops 4700897280 | bytes 24510464 | tf_op jit(solution)/shard_map/dot_general | solution.py:41
  421.1 7.8 %reshape.136 = bf16[32,10,7168]{2,1,0:T(8,128)(2,1)} reshape(bf16[320,7168]{1,0:T(8,128)(2,1)} %convolution_convert_fusion) | data formatting | bytes 9175040 | tf_op jit(solution)/shard_map/reshape | solution.py:110
  428.9 10.5 %all-to-all-start.1 = ((bf16[32,10,7168]{2,1,0:T(8,128)(2,1)}), bf16[32,10,7168]{2,1,0:T(8,128)(2,1)}, u32[]{:S(2)}, u32[]{:S(2)}) async-start(bf16[32,10,7168]{2,1,0:T(8,128)(2,1)} %reshape.136), calls=%async_computation.1 | async-start | bytes 14680064 | tf_op jit(solution)/shard_map/all_to_all | solution.py:112
  439.4 0.1 mul.70
  439.6 0.2 fusion.29
  439.8 0.2 select_reduce_fusion
  439.9 0.1 divide_reduce_fusion
  440.2 3.6 fusion.30
  443.7 0.3 fusion.10
  444.0 0.4 fusion.28
  444.5 5.1 convolution_convert_fusion.2
  449.6 156.9 %all-to-all-done.1 = bf16[32,10,7168]{2,1,0:T(8,128)(2,1)} async-done(((bf16[32,10,7168]{2,1,0:T(8,128)(2,1)}), bf16[32,10,7168]{2,1,0:T(8,128)(2,1)}, u32[]{:S(2)}, u32[]{:S(2)}) %all-to-all-start.1) | async-done | bytes 4587552 | tf_op jit(solution)/shard_map/all_to_all | solution.py:112
  606.5 10.2 %convert.1 = f32[16,2,10,7168]{3,2,1,0:T(8,128)} convert(bf16[16,2,10,7168]{3,2,1,0:T(8,128)(2,1)} %bitcast.6) | non-fusion elementwise | flops 2293760 | bytes 13762560 | tf_op jit(solution)/shard_map/convert_element_type | solution.py:113
  616.7 7.9 %fusion.2 = bf16[16,1,10,7168]{3,2,0,1:T(8,128)(2,1)} fusion(f32[16,2,10,7168]{3,2,1,0:T(8,128)} %convert.1), kind=kLoop, calls=%fused_computation.6 | loop fusion | flops 2293760 | bytes 11468800 | tf_op jit(solution)/shard_map/convert_element_type | solution.py:114
  624.6 3.2 convert_element_type.54
  627.8 3.0 gather_fusion
  630.7 3.6 multiply_reduce_fusion
  (25 shorter events, 0.5 us)
Async XLA Ops:
  7.2 433.0 %copy-start = (bf16[16,64,512]{2,1,0:T(8,128)(2,1)S(1)}, bf16[16,64,512]{2,1,0:T(8,128)(2,1)}, u32[]{:S(2)}) copy-start(bf16[16,64,512]{2,1,0:T(8,128)(2,1)} %param.15) | copy-start | bytes 3145732
  7.2 4.0 copy-start.5
  7.2 315.7 %all-gather.3.cloned.1.call-start = ((), (), s32[]{:S(2)}) async-start(), calls=%async_computation.2 | async-start | bytes 16515072 | tf_op jit(solution)/shard_map/all_gather | solution.py:86
  10.4 397.0 %all-gather.5.cloned.1.call-start = ((), (), s32[]{:S(2)}) async-start(), calls=%async_computation.3 | async-start | bytes 8257536 | tf_op jit(solution)/shard_map/all_gather | solution.py:87
  428.9 10.7 %copy-start.1 = (bf16[16,7168]{1,0:T(8,128)(2,1)S(1)}, bf16[16,7168]{1,0:T(8,128)(2,1)}, u32[]{:S(2)}) copy-start(bf16[16,7168]{1,0:T(8,128)(2,1)} %param.10) | copy-start | bytes 688132
  428.9 10.7 %copy-start.4 = (bf16[7168,16]{0,1:T(8,128)(2,1)S(1)}, bf16[7168,16]{0,1:T(8,128)(2,1)}, u32[]{:S(2)}) copy-start(bf16[7168,16]{0,1:T(8,128)(2,1)} %param.12) | copy-start | bytes 688132
  428.9 11.2 %copy-start.6 = (s32[16]{0:T(128)S(1)}, s32[16]{0:T(128)}, u32[]{:S(2)}) copy-start(s32[16]{0:T(128)} %param.19) | copy-start | bytes 196
  428.9 177.6 %all-to-all-start.1 = ((bf16[32,10,7168]{2,1,0:T(8,128)(2,1)}), bf16[32,10,7168]{2,1,0:T(8,128)(2,1)}, u32[]{:S(2)}, u32[]{:S(2)}) async-start(bf16[32,10,7168]{2,1,0:T(8,128)(2,1)} %reshape.136), calls=%async_computation.1 | async-start | bytes 14680064 | tf_op jit(solution)/shard_map/all_to_all | solution.py:112
  439.4 4.3 copy-start.2
  439.4 4.3 copy-start.3
Sparse Core Ops, SparseCore 0:
  10.6 312.3 all-gather.2
  324.7 82.6 all-gather.4
where the time goes:
time: 642 us; the launch traced here: 641 us
  waiting for transfers between devices  276 us (43%)
  blocking collectives  254 us (40%)
  matrix products  31.6 us (5%)
  local copies, waits for them, and re-layouts  31.3 us (5%)
  other arithmetic  23.1 us (4%)
  between operations  14.2 us (2%)
  starting transfers between devices  10.6 us (2%)
    all_to_all x1, blocking collectives, on_device(): lax.all_to_all(outgoing, 'exp', split_axis=0, concat_axis=0, tiled=True)  254 us
    all_to_all x1, waiting for transfers between devices, on_device(): lax.all_to_all(slice_parts, 'exp', split_axis=0, concat_axis=0, tiled=True)  157 us
    all_gather x1, waiting for transfers between devices, on_device(): lax.all_gather(down_weight, 'rep', axis=1, tiled=True)  77.4 us
    all_gather x1, waiting for transfers between devices, on_device(): lax.all_gather(gate_up, 'rep', axis=1, tiled=True)  41.4 us
    dot_general x1, matrix products, partial_output(): return jnp.dot(activated, down_weight, preferred_element_type=jnp.float32)  13.7 us
  transfers between devices with their start and end apart: 3, of which 3 were waited for; matrix products, arithmetic and copies ran while one was open for 5% of the time, Pallas kernels for 0%

commit v1 on v0

--- a/solution.py
+++ b/solution.py
@@ -7,6 +7,12 @@
 ROPE = 64
 NOPE = 128
 route_scale = 2.827
+
+
+def orders_map(local_block, along_axis):
+    return jnp.concatenate(
+        lax.all_to_all(jnp.stack([local_block] * lax.psum(1, along_axis)), along_axis, 0, 0), axis=1
+    )
 
 
 def slot_table(expert_ids, experts, capacity):
@@ -83,7 +89,7 @@
     model_width = hidden.shape[1]
     capacity = min(rows_dev, max(2, rows_dev * top_k * 5 // (4 * experts)))
     full_gate_up, full_down = (
-        lax.all_gather(gate_up, "rep", axis=1, tiled=True),
+        orders_map(gate_up, "rep"),
         lax.all_gather(down_weight, "rep", axis=1, tiled=True),
     )
     slice_gate_up = full_gate_up[0]

time: 642 us -> 700 us (1.090)
  waiting for transfers between devices: 276 us -> 545 us
  blocking collectives: 254 us -> 0 us
  starting transfers between devices: 10.6 us -> 31.6 us
  local copies, waits for them, and re-layouts: 31.3 us -> 52.2 us
    all_to_all x0 -> x2, waiting for transfers between devices: none -> 394 us  [the longest x1 231 us: orders_map(): lax.all_to_all(jnp.stack([local_block] * lax.psum(1, along_axis)), along_...]
    all_to_all x1 -> x0, blocking collectives: 254 us -> none  [on_device(): lax.all_to_all(outgoing, 'exp', split_axis=0, concat_axis=0, tiled=True)]
    all_gather x1, waiting for transfers between devices: 77.4 us -> 0.02 us  [on_device(): lax.all_gather(down_weight, 'rep', axis=1, tiled=True)]
    all_gather x1 -> x0, waiting for transfers between devices: 41.4 us -> none  [on_device(): lax.all_gather(gate_up, 'rep', axis=1, tiled=True)]
    all_to_all x0 -> x2, starting transfers between devices: none -> 17 us  [the longest x1 11.1 us: on_device(): lax.all_to_all(outgoing, 'exp', split_axis=0, concat_axis=0, tiled=True)]
    all_to_all x0 -> x1, local copies, waits for them, and re-layouts: none -> 7.9 us  [orders_map(): lax.all_to_all(jnp.stack([local_block] * lax.psum(1, along_axis)), along_...]
    another operation x0 -> x2, local copies, waits for them, and re-layouts: none -> 7.31 us  [the longest x1 5.46 us: orders_map(): jnp.stack([local_block] * lax.psum(1, along_axis))]
  transfers between devices with their start and end apart: 3 -> 4, of which waited for: 3 -> 3; matrix products, arithmetic and copies ran while one was open for 5% -> 4% of each run, Pallas kernels for 0% -> 0%
where the time goes in v1:
time: 700 us; the launch traced here: 693 us
  waiting for transfers between devices  545 us (78%)
  local copies, waits for them, and re-layouts  52.2 us (7%)
  starting transfers between devices  31.6 us (5%)
  matrix products  27.3 us (4%)
  other arithmetic  23.1 us (3%)
  between operations  14.2 us (2%)
    all_to_all x1, waiting for transfers between devices, orders_map(): lax.all_to_all(jnp.stack([local_block] * lax.psum(1, along_axis)), along_...  231 us
    all_to_all x1, waiting for transfers between devices, on_device(): lax.all_to_all(outgoing, 'exp', split_axis=0, concat_axis=0, tiled=True)  163 us
    all_to_all x1, waiting for transfers between devices, on_device(): lax.all_to_all(slice_parts, 'exp', split_axis=0, concat_axis=0, tiled=True)  150 us
    all_to_all x1, starting transfers between devices, on_device(): lax.all_to_all(slice_parts, 'exp', split_axis=0, concat_axis=0, tiled=True)  14.6 us
  transfers between devices with their start and end apart: 4, of which 3 were waited for; matrix products, arithmetic and copies ran while one was open for 4% of the time, Pallas kernels for 0%

profile of v1, /device:TPU:33, one launch (start us, length us, event | category | flops | bytes accessed | tf_op | source)
XLA Modules:
  0.0 693.3 jit_solution(10360059915854904918)
XLA Ops:
  7.2 0.8 copy.30
  8.2 0.2 reduce_window_sum.11
  8.4 0.2 select_reduce_fusion.1
  8.8 1.7 convolution_convert_fusion.1
  10.5 2.7 broadcast_in_dim.48
  13.3 5.9 broadcast_in_dim.49
  19.2 11.1 %all-to-all-start = ((bf16[32,10,7168]{2,1,0:T(8,128)(2,1)}), bf16[32,10,7168]{2,1,0:T(8,128)(2,1)}, u32[]{:S(2)}, u32[]{:S(2)}) async-start(bf16[32,10,7168]{2,1,0:T(8,128)(2,1)} %bitcast.55), calls=%async_computation | async-start | bytes 14680064 | tf_op jit(solution)/shard_map/all_to_all | solution.py:111
  30.2 1.9 copy.32
  32.1 162.6 %all-to-all-done = bf16[32,10,7168]{2,1,0:T(8,128)(2,1)} async-done(((bf16[32,10,7168]{2,1,0:T(8,128)(2,1)}), bf16[32,10,7168]{2,1,0:T(8,128)(2,1)}, u32[]{:S(2)}, u32[]{:S(2)}) %all-to-all-start) | async-done | bytes 4587552 | tf_op jit(solution)/shard_map/all_to_all | solution.py:111
  194.7 5.5 stack.2
  200.1 5.9 all-to-all-start.1
  206.1 0.7 all-gather.2.cloned.1.call-update
  206.8 8.1 %reshape.138 = bf16[320,7168]{1,0:T(8,128)(2,1)} reshape(bf16[32,10,7168]{2,1,0:T(8,128)(2,1)} %all-to-all-done) | data formatting | bytes 9175040 | tf_op jit(solution)/shard_map/reshape | solution.py:114
  214.8 231.2 %all-to-all-done.1 = bf16[8,1,64,2,7168]{4,2,3,1,0:T(8,128)(2,1)} async-done(((bf16[8,1,64,2,7168]{4,2,3,1,0:T(8,128)(2,1)}), bf16[8,1,64,2,7168]{4,2,3,1,0:T(8,128)(2,1)}, u32[]{:S(2)}, u32[]{:S(2)}) %all-to-all-start.1) | async-done | bytes 14680096 | tf_op jit(solution)/shard_map/all_to_all | solution.py:14
  446.0 7.9 %copy.33 = bf16[8,1,64,2,7168]{4,2,0,3,1:T(8,128)(2,1)S(1)} copy(bf16[8,1,64,2,7168]{4,2,3,1,0:T(8,128)(2,1)} %all-to-all-done.1) | data formatting | bytes 29360128 | tf_op jit(solution)/shard_map/all_to_all | solution.py:14
  453.9 5.2 copy-done.1
  459.1 2.6 fusion.4
  461.7 13.9 %convolution_convert_fusion = bf16[320,7168]{1,0:T(8,128)(2,1)} fusion(bf16[1,512,7168]{2,1,0:T(8,128)(2,1)} %all-gather.2.cloned.1.call-done, bf16[320,7168]{1,0:T(8,128)(2,1)} %reshape.138, bf16[512,2,7168]{2,0,1:T(8,128)(2,1)} %bitcast.57, f32[320,512]{1,0:T(8,128)S(1)} %fusion.4), kind=kOutput, calls=%fused_computation.2 | convolution fusion | flops 4700897280 | bytes 24510464 | tf_op jit(solution)/shard_map/dot_general | solution.py:47
  475.6 7.8 %reshape.139 = bf16[32,10,7168]{2,1,0:T(8,128)(2,1)} reshape(bf16[320,7168]{1,0:T(8,128)(2,1)} %convolution_convert_fusion) | data formatting | bytes 9175040 | tf_op jit(solution)/shard_map/reshape | solution.py:116
  483.4 14.6 %all-to-all-start.2 = ((bf16[32,10,7168]{2,1,0:T(8,128)(2,1)}), bf16[32,10,7168]{2,1,0:T(8,128)(2,1)}, u32[]{:S(2)}, u32[]{:S(2)}) async-start(bf16[32,10,7168]{2,1,0:T(8,128)(2,1)} %reshape.139), calls=%async_computation.2 | async-start | bytes 14680064 | tf_op jit(solution)/shard_map/all_to_all | solution.py:118
  498.2 0.2 fusion.29
  498.4 0.2 select_reduce_fusion
  498.8 3.6 fusion.30
  502.4 0.3 fusion.10
  502.7 0.4 fusion.28
  503.1 5.1 convolution_convert_fusion.2
  508.2 150.4 %all-to-all-done.2 = bf16[32,10,7168]{2,1,0:T(8,128)(2,1)} async-done(((bf16[32,10,7168]{2,1,0:T(8,128)(2,1)}), bf16[32,10,7168]{2,1,0:T(8,128)(2,1)}, u32[]{:S(2)}, u32[]{:S(2)}) %all-to-all-start.2) | async-done | bytes 4587552 | tf_op jit(solution)/shard_map/all_to_all | solution.py:118
  658.7 10.2 %convert.1 = f32[16,2,10,7168]{3,2,1,0:T(8,128)} convert(bf16[16,2,10,7168]{3,2,1,0:T(8,128)(2,1)} %bitcast.7) | non-fusion elementwise | flops 2293760 | bytes 13762560 | tf_op jit(solution)/shard_map/convert_element_type | solution.py:119
  668.9 7.9 %fusion.2 = bf16[16,1,10,7168]{3,2,0,1:T(8,128)(2,1)} fusion(f32[16,2,10,7168]{3,2,1,0:T(8,128)} %convert.1), kind=kLoop, calls=%fused_computation.6 | loop fusion | flops 2293760 | bytes 11468800 | tf_op jit(solution)/shard_map/convert_element_type | solution.py:120
  676.8 3.2 convert_element_type.54
  679.9 3.0 gather_fusion
  682.9 3.6 multiply_reduce_fusion
  (29 shorter events, 0.8 us)
Async XLA Ops:
  7.2 491.6 %copy-start = (bf16[16,64,512]{2,1,0:T(8,128)(2,1)S(1)}, bf16[16,64,512]{2,1,0:T(8,128)(2,1)}, u32[]{:S(2)}) copy-start(bf16[16,64,512]{2,1,0:T(8,128)(2,1)} %param.15) | copy-start | bytes 3145732
  19.2 175.5 %all-to-all-start = ((bf16[32,10,7168]{2,1,0:T(8,128)(2,1)}), bf16[32,10,7168]{2,1,0:T(8,128)(2,1)}, u32[]{:S(2)}, u32[]{:S(2)}) async-start(bf16[32,10,7168]{2,1,0:T(8,128)(2,1)} %bitcast.55), calls=%async_computation | async-start | bytes 14680064 | tf_op jit(solution)/shard_map/all_to_all | solution.py:111
  200.1 245.9 %all-to-all-start.1 = ((bf16[8,1,64,2,7168]{4,2,3,1,0:T(8,128)(2,1)}), bf16[8,1,64,2,7168]{4,2,3,1,0:T(8,128)(2,1)}, u32[]{:S(2)}, u32[]{:S(2)}) async-start(bf16[8,1,64,2,7168]{4,2,3,1,0:T(8,128)(2,1)} %stack.2), calls=%async_computation.1 | async-start | bytes 29360128 | tf_op jit(solution)/shard_map/all_to_all | solution.py:14
  206.1 255.7 %all-gather.2.cloned.1.call-start = ((), (), s32[]{:S(2)}) async-start(), calls=%async_computation.3 | async-start | bytes 8257536 | tf_op jit(solution)/shard_map/all_gather | solution.py:93
  446.0 13.1 %copy-start.2 = (bf16[320,7168]{1,0:T(8,128)(2,1)S(1)}, bf16[320,7168]{1,0:T(8,128)(2,1)}, u32[]{:S(2)}) copy-start(bf16[320,7168]{1,0:T(8,128)(2,1)} %reshape.138) | copy-start | bytes 13762564
  453.9 5.2 copy-start.1
  483.4 14.8 %copy-start.3 = (bf16[16,7168]{1,0:T(8,128)(2,1)S(1)}, bf16[16,7168]{1,0:T(8,128)(2,1)}, u32[]{:S(2)}) copy-start(bf16[16,7168]{1,0:T(8,128)(2,1)} %param.10) | copy-start | bytes 688132
  483.4 14.8 %copy-start.6 = (bf16[7168,16]{0,1:T(8,128)(2,1)S(1)}, bf16[7168,16]{0,1:T(8,128)(2,1)}, u32[]{:S(2)}) copy-start(bf16[7168,16]{0,1:T(8,128)(2,1)} %param.12) | copy-start | bytes 688132
  483.4 15.3 %copy-start.7 = (s32[16]{0:T(128)S(1)}, s32[16]{0:T(128)}, u32[]{:S(2)}) copy-start(s32[16]{0:T(128)} %param.19) | copy-start | bytes 196
  483.4 175.3 %all-to-all-start.2 = ((bf16[32,10,7168]{2,1,0:T(8,128)(2,1)}), bf16[32,10,7168]{2,1,0:T(8,128)(2,1)}, u32[]{:S(2)}, u32[]{:S(2)}) async-start(bf16[32,10,7168]{2,1,0:T(8,128)(2,1)} %reshape.139), calls=%async_computation.2 | async-start | bytes 14680064 | tf_op jit(solution)/shard_map/all_to_all | solution.py:118
  498.0 4.3 copy-start.4
  498.1 4.3 copy-start.5
Sparse Core Ops, SparseCore 0:
  208.7 236.7 all-gather.1
